TPU v7x, 32 devices: a whole 2x2x4 slice. The times are simulated.
32 devices in a mesh: leaf: 8 (over z, x), vec: 4 (over y, core).
Axes of the slice: x: 2, y: 2, z: 4, core: 2. Of those that a mesh axis runs over, the one named last changes fastest.
Arguments:
- vectors: float32 [32, 65536], P('vec', 'leaf'), may hold values from -15 to 15
- coords: float32 [3, 65536], P(None, 'leaf'), may hold values from 0 to 64, as said below
- leaf_basis: float32 [32, 65536], P(None, 'leaf'), may hold values from -0.375 to 0.375
- node_ops: float32 [496, 32, 128], P('leaf'), may hold values from -0.75 to 0.75
- top_ops: float32 [2, 32, 192], replicated, may hold values from -0.75 to 0.75
- near_target: int32 [1280], P('leaf'), may hold values from 0 to 255, as said below
- near_source: int32 [1280], P('leaf'), may hold values from 0 to 255, as said below
- near_count: int32 [8], P('leaf'), may hold values from 64 to 160, as said below
Outputs:
- product: float32 [32, 65536], P('vec', 'leaf')
- gram_matrix: float32 [32, 32], P(None, 'vec')
Inputs may be any that keep to these rules, and one draw needn't show every extreme that they name: `near_target`: slots of one index of leaf name target leaves of that index only; each aligned block of 32 slots of an index names each of its leaves once; in the first run every leaf is paired with itself, and in the second run the first leaf of each index is paired with the leaf just below it and the last leaf with the leaf just above it, where those exist. `near_source`: A source leaf lies within 4 leaves of its target leaf; no pair repeats within one index of leaf. The first near_count[d] slots of index d are live, the rest are padding; some index fills all 160 slots. `coords`: point k lies in the box of its leaf l = k // 256: first coordinate from 0.25 l to 0.25 (l + 1), the other two from 0 to 1.
All inputs are finite; a program needn't handle non-finite values.
Results may differ from a plain program's by a relative error of at most 0.0003.
Values sent between devices are 32-bit elements; how exact they have to be, the bound alone decides.
A program may use at most 64 MiB of HBM per device.

v0:
```python
import jax
import jax.numpy as jnp
import numpy as np
from jax import lax
from jax.sharding import PartitionSpec as P

PTS = 256
NEAR_REACH = 4
EXACT_ARITHMETIC = lax.Precision.HIGHEST
SIGNAL = 0.1
NUGGET = 0.5
LENGTH = 0.35
EVEN_OFFSETS = (-2, 2, 3)
ODD_OFFSETS = (-3, -2, 2)


def padded_2(block, sides, width):
    for axis, dim in sides:
        count = lax.axis_size(axis)
        forward = [(i, i + 1) for i in range(count - 1)]
        backward = [(target, source) for source, target in forward]
        low = lax.ppermute(
            lax.slice_in_dim(block, block.shape[dim] - width, None, axis=dim), axis, forward
        )
        high = lax.ppermute(lax.slice_in_dim(block, 0, width, axis=dim), axis, backward)
        block = jnp.concatenate([low, block, high], axis=dim)
    return block


def matern(target_pts, source_pts):
    pair_separation = jnp.zeros(
        (target_pts.shape[1], target_pts.shape[2], source_pts.shape[2]), jnp.float32
    )
    for axis_id in range(3):
        spacing = target_pts[axis_id][:, :, None] - source_pts[axis_id][:, None, :]
        pair_separation = pair_separation + spacing * spacing
    scaled = jnp.sqrt(3.0 * pair_separation) / LENGTH
    return SIGNAL * (1.0 + scaled) * jnp.exp(-scaled)


def take_rows(padded, count_nodes, pad_width):
    parity_ids = np.arange(count_nodes) % 2
    gathered = []
    for slot_index in range(3):
        shift_by = np.where(parity_ids == 0, EVEN_OFFSETS[slot_index], ODD_OFFSETS[slot_index])
        gathered.append(padded[np.arange(count_nodes) + shift_by + pad_width])
    return jnp.stack(gathered, axis=1)


def couple_level(padded, operators, count_nodes, pad_width, rank_size):
    sources = take_rows(padded, count_nodes, pad_width)
    blocks = operators[:, :, : 3 * rank_size].reshape(count_nodes, rank_size, 3, rank_size)
    return jnp.einsum("navr,nras->nvs", sources, blocks, precision=EXACT_ARITHMETIC)


def raise_level(incoming_coefficients, operators, rank_size):
    moved = jnp.einsum(
        "nvr,nrs->nvs",
        incoming_coefficients,
        operators[:, :, 3 * rank_size :],
        precision=EXACT_ARITHMETIC,
    )
    return moved[0::2] + moved[1::2]


def lower_level(field_in, operators, rank_size):
    spread = jnp.repeat(field_in, 2, axis=0)
    return jnp.einsum(
        "nvs,nrs->nvr", spread, operators[:, :, 3 * rank_size :], precision=EXACT_ARITHMETIC
    )


def through(incoming_coefficients, operators, position, rank_size):
    return jnp.einsum(
        "...r,rs->...s",
        incoming_coefficients,
        operators[:, position * rank_size : (position + 1) * rank_size],
        precision=EXACT_ARITHMETIC,
    )


def couple_top(partners, operators, parity, rank_size):
    far_left, near_left, near_right, far_right = partners
    outer = jnp.where(
        parity == 0,
        through(far_right, operators, 3, rank_size),
        through(far_left, operators, 0, rank_size),
    )
    return (
        through(near_left, operators, 1, rank_size)
        + through(near_right, operators, 2, rank_size)
        + outer
    )


def raise_pair(left_coef, right_coef, operators, rank_size):
    return through(left_coef, operators, 4, rank_size) + through(
        right_coef, operators, 5, rank_size
    )


def lower_top(field_in, operators, parity, rank_size):
    even_part = jnp.einsum(
        "...s,rs->...r",
        field_in,
        operators[:, 4 * rank_size : 5 * rank_size],
        precision=EXACT_ARITHMETIC,
    )
    odd_part = jnp.einsum(
        "...s,rs->...r",
        field_in,
        operators[:, 5 * rank_size : 6 * rank_size],
        precision=EXACT_ARITHMETIC,
    )
    return jnp.where(parity == 0, even_part, odd_part)


def near_field(window, local_coords, targets, sources, weights, pair_block):
    columns = window.shape[0] - 3
    leaves_dev = local_coords.shape[1]
    step_count = targets.shape[0] // pair_block

    def add_block(accumulated_sum, portion):
        target_ids, source_ids, live_mask = portion
        source_rows = jnp.take(window, source_ids, axis=1)
        target_pts = jnp.take(local_coords, target_ids, axis=1)
        kernel = matern(target_pts, source_rows[columns:])
        contribution = jnp.einsum(
            "vbs,bts->bvt", source_rows[:columns], kernel, precision=EXACT_ARITHMETIC
        )
        selection_mask = (target_ids[:, None] == jnp.arange(leaves_dev)[None, :]).astype(
            jnp.float32
        ) * live_mask[:, None]
        return (
            accumulated_sum
            + jnp.einsum("qs,qhg->hsg", selection_mask, contribution, precision=EXACT_ARITHMETIC),
            None,
        )

    initial = jnp.zeros((columns, leaves_dev, window.shape[2]), jnp.float32)
    portions = (
        targets.reshape(step_count, pair_block),
        sources.reshape(step_count, pair_block),
        weights.reshape(step_count, pair_block),
    )
    accumulated_sum, unused = lax.scan(add_block, initial, portions)
    return accumulated_sum.reshape(columns, leaves_dev * window.shape[2])


def on_device(vectors, coords, leaf_basis, node_ops, top_ops, near_target, near_source, near_count):
    rank_size = leaf_basis.shape[0]
    columns_dev = vectors.shape[0]
    points_dev = vectors.shape[1]
    leaves_dev = points_dev // PTS
    device = lax.axis_index("leaf")
    vec_index = lax.axis_index("vec")
    vec_count = lax.axis_size("vec")
    leaf_count = lax.axis_size("leaf")
    all_columns = lax.all_gather(vectors, "vec", axis=0, tiled=True)
    base_leaf = device * leaves_dev
    slot_ids = jnp.arange(near_target.shape[0], dtype=jnp.int32)
    live_all = (slot_ids < near_count[0]).astype(jnp.float32)
    target_all = near_target - base_leaf
    source_all = near_source - base_leaf + NEAR_REACH
    local_coords = coords.reshape(3, leaves_dev, PTS)
    stacked = jnp.concatenate([all_columns, coords], axis=0)
    window = padded_2(stacked, (("leaf", 1),), NEAR_REACH * PTS)
    window = window.reshape(all_columns.shape[0] + 3, leaves_dev + 2 * NEAR_REACH, PTS)
    share_count = near_target.shape[0] // vec_count
    slot_grid = slot_ids.reshape(share_count, vec_count)
    picked = lax.dynamic_slice_in_dim(slot_grid, vec_index, 1, 1)[:, 0]
    partial_sum = near_field(
        window,
        local_coords,
        target_all[picked],
        source_all[picked],
        live_all[picked],
        share_count // (leaves_dev // vec_count),
    )
    near_part = lax.psum_scatter(partial_sum, "vec", scatter_dimension=0, tiled=True)
    leaf_basis_matrix = leaf_basis.reshape(rank_size, leaves_dev, PTS)
    current = jnp.einsum(
        "vlp,rlp->lvr",
        vectors.reshape(columns_dev, leaves_dev, PTS),
        leaf_basis_matrix,
        precision=EXACT_ARITHMETIC,
    )
    level_ops = []
    level_fields = []
    offset_node = 0
    nodes_here = leaves_dev
    while nodes_here >= 2:
        ops_here = node_ops[offset_node : offset_node + nodes_here]
        rim_width = min(3, nodes_here)
        padded = padded_2(current, (("leaf", 0),), rim_width)
        level_fields.append(couple_level(padded, ops_here, nodes_here, rim_width, rank_size))
        level_ops.append(ops_here)
        current = raise_level(current, ops_here, rank_size)
        offset_node += nodes_here
        nodes_here //= 2
    top_levels = top_ops.shape[0]
    top_fields = []
    all_roots = lax.all_gather(current, "leaf", axis=0, tiled=True)
    for height in range(top_levels):
        padded_top = jnp.pad(all_roots, ((3, 3), (0, 0), (0, 0)))
        node_id = device // (1 << height)
        near_rows = lax.dynamic_slice_in_dim(padded_top, node_id, 7, 0)
        partners = (near_rows[0], near_rows[1], near_rows[5], near_rows[6])
        top_fields.append(couple_top(partners, top_ops[height], node_id % 2, rank_size))
        if height + 1 < top_levels:
            all_roots = raise_pair(all_roots[0::2], all_roots[1::2], top_ops[height], rank_size)
    downward = top_fields[top_levels - 1]
    for height in range(top_levels - 2, -1, -1):
        parity = device // (1 << height) % 2
        downward = top_fields[height] + lower_top(downward, top_ops[height], parity, rank_size)
    downward = downward[None]
    for index_level in range(len(level_fields) - 1, -1, -1):
        downward = level_fields[index_level] + lower_level(
            downward, level_ops[index_level], rank_size
        )
    far_part = jnp.einsum(
        "lvr,rlp->vlp", downward, leaf_basis_matrix, precision=EXACT_ARITHMETIC
    ).reshape(columns_dev, points_dev)
    product = near_part + far_part + NUGGET * vectors
    gram_part = jnp.einsum("ip,jp->ij", all_columns, product, precision=EXACT_ARITHMETIC)
    gram_matrix = lax.psum(gram_part, "leaf") / (leaf_count * points_dev)
    return (product, gram_matrix)


def solution(mesh):
    return jax.shard_map(
        on_device,
        mesh=mesh,
        in_specs=(
            P("vec", "leaf"),
            P(None, "leaf"),
            P(None, "leaf"),
            P("leaf", None, None),
            P(),
            P("leaf"),
            P("leaf"),
            P("leaf"),
        ),
        out_specs=(P("vec", "leaf"), P(None, "vec")),
        check_vma=False,
    )
```

profile of v0, /device:TPU:0, one launch (start us, length us, event | category | flops | bytes accessed | tf_op | source)
XLA Modules:
  0.0 216.0 jit_solution(17568019953974837203)
XLA Ops:
  7.2 2.3 %fusion.55 = f32[32,8,32]{2,1,0:T(8,128)S(1)} fusion(f32[8,32,256]{2,0,1:T(8,128)} %bitcast.178, f32[4,32,8,256]{3,2,1,0:T(8,128)} %bitcast.175), kind=kOutput, calls=%fused_computation.110 | convolution fusion | flops 25165824 | bytes 1343488 | tf_op jit(solution)/shard_map/vlp,rlp->lvr/dot_general | solution.py:182
  11.4 4.9 %collective-permute-start.10 = (f32[2,8,32]{2,1,0:T(8,128)S(1)}, f32[2,8,32]{2,1,0:T(8,128)S(1)}, u32[]{:S(2)}, u32[]{:S(2)}) collective-permute-start(f32[2,8,32]{2,1,0:T(8,128)S(1)} %slice_add_fusion.3), channel_id=1, source_target_pairs={{0,4},{4,8},{8,12},{12,16},{16,20},{20,24},{24,28},{1,5},{5,9},{9,... | collective-permute-start | bytes 6152 | tf_op jit(solution)/shard_map/ppermute | solution.py:22
  16.3 1.3 collective-permute-start.11
  18.3 5.1 %collective-permute-start.8 = (f32[3,8,32]{2,1,0:T(8,128)}, f32[3,8,32]{2,1,0:T(8,128)}, u32[]{:S(2)}, u32[]{:S(2)}) collective-permute-start(f32[3,8,32]{2,1,0:T(8,128)} %get-tuple-element.113), channel_id=1, source_target_pairs={{0,4},{4,8},{8,12},{12,16},{16,20},{20,24},{24,28},{1,5},{5,9},{9,... | collective-permute-start | bytes 9224 | tf_op jit(solution)/shard_map/ppermute | solution.py:22
  24.0 4.4 %collective-permute-start.6 = (f32[3,8,32]{2,1,0:T(8,128)}, f32[3,8,32]{2,1,0:T(8,128)}, u32[]{:S(2)}, u32[]{:S(2)}) collective-permute-start(f32[3,8,32]{2,1,0:T(8,128)} %get-tuple-element.111), channel_id=1, source_target_pairs={{0,4},{4,8},{8,12},{12,16},{16,20},{20,24},{24,28},{1,5},{5,9},{9,... | collective-permute-start | bytes 9224 | tf_op jit(solution)/shard_map/ppermute | solution.py:22
  29.9 31.5 %all_gather.7 = f32[8,8,32]{2,1,0:T(8,128)S(1)} all-gather(f32[1,8,32]{2,1,0:T(8,128)S(1)} %slice_add_fusion.4), channel_id=1, replica_groups=mesh['leaf'=8,'vec'=4] {'leaf'}, dimensions={0}, use_global_device_ids=true | all-gather | bytes 9216 | tf_op jit(solution)/shard_map/all_gather | solution.py:203
  72.6 1.4 reshape.158
  74.0 1.7 reshape.157
  78.4 1.6 collective-permute-start.4
  83.5 1.3 constant_dynamic-update-slice_fusion.1
  84.9 4.6 %collective-permute-start = (f32[35,1024]{1,0:T(8,128)S(1)}, f32[35,1024]{1,0:T(8,128)S(1)}, u32[]{:S(2)}, u32[]{:S(2)}) collective-permute-start(f32[35,1024]{1,0:T(8,128)S(1)} %get-tuple-element.103), channel_id=1, source_target_pairs={{0,4},{4,8},{8,12},{12,16},{16,20},{20,24},{24,28},{1,5},{5,9},{9,... | collective-permute-start | bytes 430088 | tf_op jit(solution)/shard_map/ppermute | solution.py:22
  92.9 5.2 %collective-permute-start.2 = (f32[3,8,32]{2,1,0:T(8,128)}, f32[3,8,32]{2,1,0:T(8,128)S(1)}, u32[]{:S(2)}, u32[]{:S(2)}) collective-permute-start(f32[3,8,32]{2,1,0:T(8,128)} %get-tuple-element.105), channel_id=1, source_target_pairs={{0,4},{4,8},{8,12},{12,16},{16,20},{20,24},{24,28},{1,5},{5,9},{9,... | collective-permute-start | bytes 9224 | tf_op jit(solution)/shard_map/ppermute | solution.py:22
  100.1 1.7 copy.66
  101.8 53.4 %while.11 = (s32[]{:T(128)}, f32[32,32,256]{2,1,0:T(8,128)S(1)}, s32[8,5]{1,0:T(8,128)S(1)}, f32[35,40,256]{2,0,1:T(8,128)}, s32[8,5]{1,0:T(8,128)S(1)}, /*index...) while((s32[]{:T(128)}, f32[32,32,256]{2,1,0:T(8,128)S(1)}, ...), condition=%wide.region_1.2_spmd.clone, body=%wide.region_0.1_spmd.clone.sunk | while | flops 146720672 | bytes 3547571 | solution.py:146
  101.8 2.0 gather_fusion
  104.7 2.4 %fusion.205 = f32[5,32,256]{2,1,0:T(8,128)S(1)} fusion(f32[5,256]{1,0:T(8,128)S(1)} %bitcast.189, f32[5,256]{1,0:T(8,128)S(1)} %bitcast.192, f32[5,256]{1,0:T(8,128)S(1)} %bitcast.190, f32[5,256]{1,0:T(8,128)S(1)} %bitcast.193, f32[5,256]{1,0:T(8,128)S(1)} %bitcast.191, f32[5,256]{1,0:T(8,128)S(1)} %bitcast.194, ...), kind=kOutput, calls=%fused_computation.22.clone.1 | convolution fusion | flops 130416640 | bytes 376832 | tf_op jit(solution)/shard_map/while/body/eval_jaxpr/vbs,bts->bvt/dot_general | solution.py:128
  107.1 1.3 fusion.207
  108.5 2.0 gather_fusion
  111.4 2.4 %fusion.205 = f32[5,32,256]{2,1,0:T(8,128)S(1)} fusion(f32[5,256]{1,0:T(8,128)S(1)} %bitcast.189, f32[5,256]{1,0:T(8,128)S(1)} %bitcast.192, f32[5,256]{1,0:T(8,128)S(1)} %bitcast.190, f32[5,256]{1,0:T(8,128)S(1)} %bitcast.193, f32[5,256]{1,0:T(8,128)S(1)} %bitcast.191, f32[5,256]{1,0:T(8,128)S(1)} %bitcast.194, ...), kind=kOutput, calls=%fused_computation.22.clone.1 | convolution fusion | flops 130416640 | bytes 376832 | tf_op jit(solution)/shard_map/while/body/eval_jaxpr/vbs,bts->bvt/dot_general | solution.py:128
  113.8 1.3 fusion.207
  115.2 2.0 gather_fusion
  118.0 2.4 %fusion.205 = f32[5,32,256]{2,1,0:T(8,128)S(1)} fusion(f32[5,256]{1,0:T(8,128)S(1)} %bitcast.189, f32[5,256]{1,0:T(8,128)S(1)} %bitcast.192, f32[5,256]{1,0:T(8,128)S(1)} %bitcast.190, f32[5,256]{1,0:T(8,128)S(1)} %bitcast.193, f32[5,256]{1,0:T(8,128)S(1)} %bitcast.191, f32[5,256]{1,0:T(8,128)S(1)} %bitcast.194, ...), kind=kOutput, calls=%fused_computation.22.clone.1 | convolution fusion | flops 130416640 | bytes 376832 | tf_op jit(solution)/shard_map/while/body/eval_jaxpr/vbs,bts->bvt/dot_general | solution.py:128
  120.5 1.3 fusion.207
  121.8 2.0 gather_fusion
  124.7 2.4 %fusion.205 = f32[5,32,256]{2,1,0:T(8,128)S(1)} fusion(f32[5,256]{1,0:T(8,128)S(1)} %bitcast.189, f32[5,256]{1,0:T(8,128)S(1)} %bitcast.192, f32[5,256]{1,0:T(8,128)S(1)} %bitcast.190, f32[5,256]{1,0:T(8,128)S(1)} %bitcast.193, f32[5,256]{1,0:T(8,128)S(1)} %bitcast.191, f32[5,256]{1,0:T(8,128)S(1)} %bitcast.194, ...), kind=kOutput, calls=%fused_computation.22.clone.1 | convolution fusion | flops 130416640 | bytes 376832 | tf_op jit(solution)/shard_map/while/body/eval_jaxpr/vbs,bts->bvt/dot_general | solution.py:128
  127.1 1.3 fusion.207
  128.5 2.0 gather_fusion
  131.4 2.4 %fusion.205 = f32[5,32,256]{2,1,0:T(8,128)S(1)} fusion(f32[5,256]{1,0:T(8,128)S(1)} %bitcast.189, f32[5,256]{1,0:T(8,128)S(1)} %bitcast.192, f32[5,256]{1,0:T(8,128)S(1)} %bitcast.190, f32[5,256]{1,0:T(8,128)S(1)} %bitcast.193, f32[5,256]{1,0:T(8,128)S(1)} %bitcast.191, f32[5,256]{1,0:T(8,128)S(1)} %bitcast.194, ...), kind=kOutput, calls=%fused_computation.22.clone.1 | convolution fusion | flops 130416640 | bytes 376832 | tf_op jit(solution)/shard_map/while/body/eval_jaxpr/vbs,bts->bvt/dot_general | solution.py:128
  133.8 1.3 fusion.207
  135.2 2.0 gather_fusion
  138.1 2.4 %fusion.205 = f32[5,32,256]{2,1,0:T(8,128)S(1)} fusion(f32[5,256]{1,0:T(8,128)S(1)} %bitcast.189, f32[5,256]{1,0:T(8,128)S(1)} %bitcast.192, f32[5,256]{1,0:T(8,128)S(1)} %bitcast.190, f32[5,256]{1,0:T(8,128)S(1)} %bitcast.193, f32[5,256]{1,0:T(8,128)S(1)} %bitcast.191, f32[5,256]{1,0:T(8,128)S(1)} %bitcast.194, ...), kind=kOutput, calls=%fused_computation.22.clone.1 | convolution fusion | flops 130416640 | bytes 376832 | tf_op jit(solution)/shard_map/while/body/eval_jaxpr/vbs,bts->bvt/dot_general | solution.py:128
  140.5 1.3 fusion.207
  141.9 2.0 gather_fusion
  144.7 2.4 %fusion.205 = f32[5,32,256]{2,1,0:T(8,128)S(1)} fusion(f32[5,256]{1,0:T(8,128)S(1)} %bitcast.189, f32[5,256]{1,0:T(8,128)S(1)} %bitcast.192, f32[5,256]{1,0:T(8,128)S(1)} %bitcast.190, f32[5,256]{1,0:T(8,128)S(1)} %bitcast.193, f32[5,256]{1,0:T(8,128)S(1)} %bitcast.191, f32[5,256]{1,0:T(8,128)S(1)} %bitcast.194, ...), kind=kOutput, calls=%fused_computation.22.clone.1 | convolution fusion | flops 130416640 | bytes 376832 | tf_op jit(solution)/shard_map/while/body/eval_jaxpr/vbs,bts->bvt/dot_general | solution.py:128
  147.2 1.3 fusion.207
  148.6 2.0 gather_fusion
  151.4 2.4 %fusion.205 = f32[5,32,256]{2,1,0:T(8,128)S(1)} fusion(f32[5,256]{1,0:T(8,128)S(1)} %bitcast.189, f32[5,256]{1,0:T(8,128)S(1)} %bitcast.192, f32[5,256]{1,0:T(8,128)S(1)} %bitcast.190, f32[5,256]{1,0:T(8,128)S(1)} %bitcast.193, f32[5,256]{1,0:T(8,128)S(1)} %bitcast.191, f32[5,256]{1,0:T(8,128)S(1)} %bitcast.194, ...), kind=kOutput, calls=%fused_computation.22.clone.1 | convolution fusion | flops 130416640 | bytes 376832 | tf_op jit(solution)/shard_map/while/body/eval_jaxpr/vbs,bts->bvt/dot_general | solution.py:128
  153.9 1.3 fusion.207
  155.2 1.6 copy.82
  164.8 1.3 gather_fusion.10
  166.1 1.3 gather_fusion.9
  167.4 1.3 gather_fusion.8
  170.2 1.4 gather_fusion.5
  171.5 1.4 convolution_bitcast_fusion.3
  172.9 1.8 convolution_bitcast_fusion.2
  174.8 3.2 %fusion.46 = f32[32,8,32]{2,1,0:T(8,128)S(1)} fusion(f32[32,32,3,32]{3,2,1,0:T(4,128)S(1)} %copy-done.1, f32[32,1,8,32]{3,2,0,1:T(8,128)S(1)} %bitcast.181, f32[32,1,8,32]{3,2,0,1:T(8,128)S(1)} %bitcast.180, f32[32,1,8,32]{3,2,0,1:T(8,128)} %bitcast.182), kind=kOutput, calls=%fused_computation.89 | convolution fusion | flops 9486336 | bytes 524288 | tf_op jit(solution)/shard_map/navr,nras->nvs/dot_general | solution.py:53
  182.2 3.1 %reduce-scatter.2.cloned.1.call-done = f32[8,8192]{1,0:T(8,128)} async-done(((f32[32,8192]{1,0:T(8,128)}), f32[8,8192]{1,0:T(8,128)}) %reduce-scatter.2.cloned.1.call-update) | async-done | bytes 262160 | tf_op jit(solution)/shard_map/reduce_scatter | solution.py:180
  187.2 21.4 %psum.7 = f32[32,8]{0,1:T(8,128)S(1)} all-reduce(f32[32,8]{0,1:T(8,128)S(1)} %convolution_bitcast_fusion.5), channel_id=1, replica_groups=mesh['leaf'=8,'vec'=4] {'leaf'}, use_global_device_ids=true, to_apply=%region_3.4 | all-reduce | flops 256 | bytes 2048 | tf_op jit(solution)/shard_map/psum | solution.py:226
  (301 shorter events, 49.1 us)
Async XLA Ops:
  7.2 2.4 %copy-start = (f32[62,32,128]{2,1,0:T(8,128)S(1)}, f32[62,32,128]{2,1,0:T(8,128)}, u32[]{:S(2)}) copy-start(f32[62,32,128]{2,1,0:T(8,128)} %param.43) | copy-start | bytes 3047428
  7.2 76.3 %all-gather.2.cloned.1.call-start = ((), (), s32[]{:S(2)}) async-start(), calls=%async_computation.1 | async-start | bytes 1310720 | tf_op jit(solution)/shard_map/all_gather | solution.py:159
  9.5 51.9 %copy-start.11 = (f32[2,32,192]{2,1,0:T(8,128)S(1)}, f32[2,32,192]{2,1,0:T(8,128)}, u32[]{:S(2)}) copy-start(f32[2,32,192]{2,1,0:T(8,128)} %param.44) | copy-start | bytes 147460
  9.6 53.6 %copy-start.27 = (s32[4]{0:T(128)S(1)}, s32[4]{0:T(128)}, u32[]{:S(2)}) copy-start(s32[4]{0:T(128)} %constant.214) | copy-start | bytes 52
  9.6 54.2 %copy-start.26 = (s32[8]{0:T(128)S(1)}, s32[8]{0:T(128)}, u32[]{:S(2)}) copy-start(s32[8]{0:T(128)} %constant.211) | copy-start | bytes 100
  9.6 54.8 %copy-start.25 = (s32[16]{0:T(128)S(1)}, s32[16]{0:T(128)}, u32[]{:S(2)}) copy-start(s32[16]{0:T(128)} %constant.208) | copy-start | bytes 196
  9.6 55.4 %copy-start.24 = (s32[32]{0:T(128)S(1)}, s32[32]{0:T(128)}, u32[]{:S(2)}) copy-start(s32[32]{0:T(128)} %constant.205) | copy-start | bytes 388
  10.3 56.1 %copy-start.23 = (s32[2]{0:T(128)S(1)}, s32[2]{0:T(128)}, u32[]{:S(2)}) copy-start(s32[2]{0:T(128)} %constant.217) | copy-start | bytes 28
  10.3 56.1 %copy-start.21 = (s32[4]{0:T(128)S(1)}, s32[4]{0:T(128)}, u32[]{:S(2)}) copy-start(s32[4]{0:T(128)} %constant.215) | copy-start | bytes 52
  10.3 56.1 %copy-start.22 = (s32[4]{0:T(128)S(1)}, s32[4]{0:T(128)}, u32[]{:S(2)}) copy-start(s32[4]{0:T(128)} %constant.216) | copy-start | bytes 52
  10.3 56.7 %copy-start.19 = (s32[8]{0:T(128)S(1)}, s32[8]{0:T(128)}, u32[]{:S(2)}) copy-start(s32[8]{0:T(128)} %constant.212) | copy-start | bytes 100
  10.3 56.7 %copy-start.20 = (s32[8]{0:T(128)S(1)}, s32[8]{0:T(128)}, u32[]{:S(2)}) copy-start(s32[8]{0:T(128)} %constant.213) | copy-start | bytes 100
  10.3 57.3 %copy-start.17 = (s32[16]{0:T(128)S(1)}, s32[16]{0:T(128)}, u32[]{:S(2)}) copy-start(s32[16]{0:T(128)} %constant.209) | copy-start | bytes 196
  10.3 57.3 %copy-start.18 = (s32[16]{0:T(128)S(1)}, s32[16]{0:T(128)}, u32[]{:S(2)}) copy-start(s32[16]{0:T(128)} %constant.210) | copy-start | bytes 196
  10.4 57.9 %copy-start.15 = (s32[32]{0:T(128)S(1)}, s32[32]{0:T(128)}, u32[]{:S(2)}) copy-start(s32[32]{0:T(128)} %constant.206) | copy-start | bytes 388
  10.4 57.9 %copy-start.16 = (s32[32]{0:T(128)S(1)}, s32[32]{0:T(128)}, u32[]{:S(2)}) copy-start(s32[32]{0:T(128)} %constant.207) | copy-start | bytes 388
  10.4 58.5 %copy-start.13 = (s32[160]{0:T(256)S(1)}, s32[160]{0:T(256)}, u32[]{:S(2)}) copy-start(s32[160]{0:T(256)} %param.46) | copy-start | bytes 1924
  10.4 58.5 %copy-start.14 = (s32[160]{0:T(256)S(1)}, s32[160]{0:T(256)}, u32[]{:S(2)}) copy-start(s32[160]{0:T(256)} %param.45) | copy-start | bytes 1924
  11.4 67.0 %collective-permute-start.10 = (f32[2,8,32]{2,1,0:T(8,128)S(1)}, f32[2,8,32]{2,1,0:T(8,128)S(1)}, u32[]{:S(2)}, u32[]{:S(2)}) collective-permute-start(f32[2,8,32]{2,1,0:T(8,128)S(1)} %slice_add_fusion.3), channel_id=1, source_target_pairs={{0,4},{4,8},{8,12},{12,16},{16,20},{20,24},{24,28},{1,5},{5,9},{9,... | collective-permute-start | bytes 6152 | tf_op jit(solution)/shard_map/ppermute | solution.py:22
  16.3 63.7 %collective-permute-start.11 = (f32[2,8,32]{2,1,0:T(8,128)S(1)}, f32[2,8,32]{2,1,0:T(8,128)S(1)}, u32[]{:S(2)}, u32[]{:S(2)}) collective-permute-start(f32[2,8,32]{2,1,0:T(8,128)S(1)} %slice_add_fusion.3), channel_id=1, source_target_pairs={{4,0},{8,4},{12,8},{16,12},{20,16},{24,20},{28,24},{5,1},{9,5},{13... | collective-permute-start | bytes 6152 | tf_op jit(solution)/shard_map/ppermute | solution.py:25
  17.6 167.6 %reduce-scatter.2.cloned.1.call-start = ((), (), s32[]{:S(2)}) async-start(), calls=%async_computation.2 | async-start | bytes 1310720 | tf_op jit(solution)/shard_map/reduce_scatter | solution.py:180
  18.3 138.5 %collective-permute-start.8 = (f32[3,8,32]{2,1,0:T(8,128)}, f32[3,8,32]{2,1,0:T(8,128)}, u32[]{:S(2)}, u32[]{:S(2)}) collective-permute-start(f32[3,8,32]{2,1,0:T(8,128)} %get-tuple-element.113), channel_id=1, source_target_pairs={{0,4},{4,8},{8,12},{12,16},{16,20},{20,24},{24,28},{1,5},{5,9},{9,... | collective-permute-start | bytes 9224 | tf_op jit(solution)/shard_map/ppermute | solution.py:22
  24.0 60.9 %collective-permute-start.6 = (f32[3,8,32]{2,1,0:T(8,128)}, f32[3,8,32]{2,1,0:T(8,128)}, u32[]{:S(2)}, u32[]{:S(2)}) collective-permute-start(f32[3,8,32]{2,1,0:T(8,128)} %get-tuple-element.111), channel_id=1, source_target_pairs={{0,4},{4,8},{8,12},{12,16},{16,20},{20,24},{24,28},{1,5},{5,9},{9,... | collective-permute-start | bytes 9224 | tf_op jit(solution)/shard_map/ppermute | solution.py:22
  28.4 61.1 %collective-permute-start.7 = (f32[3,8,32]{2,1,0:T(8,128)}, f32[3,8,32]{2,1,0:T(8,128)}, u32[]{:S(2)}, u32[]{:S(2)}) collective-permute-start(f32[3,8,32]{2,1,0:T(8,128)} %get-tuple-element.112), channel_id=1, source_target_pairs={{4,0},{8,4},{12,8},{16,12},{20,16},{24,20},{28,24},{5,1},{9,5},{13... | collective-permute-start | bytes 9224 | tf_op jit(solution)/shard_map/ppermute | solution.py:25
  78.3 6.5 %copy-start.7 = (f32[3,8192]{1,0:T(4,128)S(1)}, f32[3,8192]{1,0:T(4,128)}, u32[]{:S(2)}) copy-start(f32[3,8192]{1,0:T(4,128)} %param.41) | copy-start | bytes 294916
  78.4 13.2 %collective-permute-start.4 = (f32[3,8,32]{2,1,0:T(8,128)}, f32[3,8,32]{2,1,0:T(8,128)S(1)}, u32[]{:S(2)}, u32[]{:S(2)}) collective-permute-start(f32[3,8,32]{2,1,0:T(8,128)} %get-tuple-element.107), channel_id=1, source_target_pairs={{0,4},{4,8},{8,12},{12,16},{16,20},{20,24},{24,28},{1,5},{5,9},{9,... | collective-permute-start | bytes 9224 | tf_op jit(solution)/shard_map/ppermute | solution.py:22
  80.0 12.9 %collective-permute-start.5 = (f32[3,8,32]{2,1,0:T(8,128)}, f32[3,8,32]{2,1,0:T(8,128)S(1)}, u32[]{:S(2)}, u32[]{:S(2)}) collective-permute-start(f32[3,8,32]{2,1,0:T(8,128)} %get-tuple-element.108), channel_id=1, source_target_pairs={{4,0},{8,4},{12,8},{16,12},{20,16},{24,20},{28,24},{5,1},{9,5},{13... | collective-permute-start | bytes 9224 | tf_op jit(solution)/shard_map/ppermute | solution.py:25
  83.5 8.1 %copy-start.12 = (f32[3,8,32]{2,1,0:T(8,128)S(1)}, f32[3,8,32]{2,1,0:T(8,128)}, u32[]{:S(2)}) copy-start(f32[3,8,32]{2,1,0:T(8,128)} %get-tuple-element.114) | copy-start | bytes 9220
  84.9 13.1 %collective-permute-start = (f32[35,1024]{1,0:T(8,128)S(1)}, f32[35,1024]{1,0:T(8,128)S(1)}, u32[]{:S(2)}, u32[]{:S(2)}) collective-permute-start(f32[35,1024]{1,0:T(8,128)S(1)} %get-tuple-element.103), channel_id=1, source_target_pairs={{0,4},{4,8},{8,12},{12,16},{16,20},{20,24},{24,28},{1,5},{5,9},{9,... | collective-permute-start | bytes 430088 | tf_op jit(solution)/shard_map/ppermute | solution.py:22
  89.5 9.9 %collective-permute-start.1 = (f32[35,1024]{1,0:T(8,128)S(1)}, f32[35,1024]{1,0:T(8,128)S(1)}, u32[]{:S(2)}, u32[]{:S(2)}) collective-permute-start(f32[35,1024]{1,0:T(8,128)S(1)} %get-tuple-element.104), channel_id=1, source_target_pairs={{4,0},{8,4},{12,8},{16,12},{20,16},{24,20},{28,24},{5,1},{9,5},{13... | collective-permute-start | bytes 430088 | tf_op jit(solution)/shard_map/ppermute | solution.py:25
  91.6 65.3 %collective-permute-start.9 = (f32[3,8,32]{2,1,0:T(8,128)S(1)}, f32[3,8,32]{2,1,0:T(8,128)S(1)}, u32[]{:S(2)}, u32[]{:S(2)}) collective-permute-start(f32[3,8,32]{2,1,0:T(8,128)S(1)} %copy-done.12), channel_id=1, source_target_pairs={{4,0},{8,4},{12,8},{16,12},{20,16},{24,20},{28,24},{5,1},{9,5},{13... | collective-permute-start | bytes 9224 | tf_op jit(solution)/shard_map/ppermute | solution.py:25
  92.9 75.9 %collective-permute-start.2 = (f32[3,8,32]{2,1,0:T(8,128)}, f32[3,8,32]{2,1,0:T(8,128)S(1)}, u32[]{:S(2)}, u32[]{:S(2)}) collective-permute-start(f32[3,8,32]{2,1,0:T(8,128)} %get-tuple-element.105), channel_id=1, source_target_pairs={{0,4},{4,8},{8,12},{12,16},{16,20},{20,24},{24,28},{1,5},{5,9},{9,... | collective-permute-start | bytes 9224 | tf_op jit(solution)/shard_map/ppermute | solution.py:22
  98.1 70.6 %collective-permute-start.3 = (f32[3,8,32]{2,1,0:T(8,128)}, f32[3,8,32]{2,1,0:T(8,128)S(1)}, u32[]{:S(2)}, u32[]{:S(2)}) collective-permute-start(f32[3,8,32]{2,1,0:T(8,128)} %get-tuple-element.106), channel_id=1, source_target_pairs={{4,0},{8,4},{12,8},{16,12},{20,16},{24,20},{28,24},{5,1},{9,5},{13... | collective-permute-start | bytes 9224 | tf_op jit(solution)/shard_map/ppermute | solution.py:25
  157.6 17.1 %copy-start.1 = (f32[32,32,3,32]{3,2,1,0:T(4,128)S(1)}, f32[32,32,3,32]{3,2,1,0:T(4,128)}, u32[]{:S(2)}) copy-start(f32[32,32,3,32]{3,2,1,0:T(4,128)} %reshape.157) | copy-start | bytes 1179652
  174.7 4.6 %copy-start.4 = (f32[16,32,3,32]{3,2,1,0:T(4,128)S(1)}, f32[16,32,3,32]{3,2,1,0:T(4,128)}, u32[]{:S(2)}) copy-start(f32[16,32,3,32]{3,2,1,0:T(4,128)} %reshape.158) | copy-start | bytes 589828
  174.7 4.5 %copy-start.8 = (f32[16,8,32]{2,1,0:T(8,128)S(1)}, f32[16,8,32]{2,1,0:T(8,128)}, u32[]{:S(2)}) copy-start(f32[16,8,32]{2,1,0:T(8,128)} %gather_fusion.10) | copy-start | bytes 49156
  174.7 4.5 %copy-start.9 = (f32[16,8,32]{2,1,0:T(8,128)S(1)}, f32[16,8,32]{2,1,0:T(8,128)}, u32[]{:S(2)}) copy-start(f32[16,8,32]{2,1,0:T(8,128)} %gather_fusion.9) | copy-start | bytes 49156
  174.7 4.5 %copy-start.10 = (f32[16,8,32]{2,1,0:T(8,128)S(1)}, f32[16,8,32]{2,1,0:T(8,128)}, u32[]{:S(2)}) copy-start(f32[16,8,32]{2,1,0:T(8,128)} %gather_fusion.8) | copy-start | bytes 49156
  178.7 2.9 %copy-start.3 = (f32[32,8192]{1,0:T(8,128)S(1)}, f32[32,8192]{1,0:T(8,128)}, u32[]{:S(2)}) copy-start(f32[32,8192]{1,0:T(8,128)} %param.42) | copy-start | bytes 3145732
  180.5 4.8 %copy-start.5 = (f32[8,8192]{1,0:T(8,128)S(1)}, f32[8,8192]{1,0:T(8,128)}, u32[]{:S(2)}) copy-start(f32[8,8192]{1,0:T(8,128)} %param.40) | copy-start | bytes 786436
  181.5 4.7 %copy-start.2 = (f32[32,8192]{1,0:T(8,128)S(1)}, f32[32,8192]{1,0:T(8,128)}, u32[]{:S(2)}) copy-start(f32[32,8192]{1,0:T(8,128)} %all-gather.2.cloned.1.call-done) | copy-start | bytes 3145732
  186.3 22.9 %copy-start.6 = (f32[8,8192]{1,0:T(8,128)}, f32[8,8192]{1,0:T(8,128)S(1)}, u32[]{:S(2)}) copy-start(f32[8,8192]{1,0:T(8,128)S(1)} %multiply_add_fusion) | copy-start | bytes 786436
Sparse Core Ops, SparseCore 0:
  17.8 19.0 all-gather.1
  157.0 28.2 reduce-scatter.1
where the time goes:
time: 217 us; the launch traced here: 216 us
  blocking collectives  52.8 us (24%)
  local copies, waits for them, and re-layouts  52.2 us (24%)
  matrix products  48 us (22%)
  starting transfers between devices  33.5 us (15%)
  between operations  15.5 us (7%)
  other arithmetic  9.62 us (4%)
  waiting for transfers between devices  3.15 us (1%)
    all_gather x1, blocking collectives, on_device(): all_roots = lax.all_gather(current, 'leaf', axis=0, tiled=True)  31.5 us
    ppermute x6, starting transfers between devices, padded_2(): lax.ppermute(lax.slice_in_dim(block, block.shape[dim] - width, None, axis...  25.7 us
    psum x1, blocking collectives, on_device(): gram_matrix = lax.psum(gram_part, 'leaf') / (leaf_count * points_dev)  21.4 us
    dot_general x8, matrix products, add_block(): jnp.einsum('vbs,bts->bvt', source_rows[:columns], kernel, precision=EXACT...  19.2 us
    gather x8, local copies, waits for them, and re-layouts, add_block(): source_rows = jnp.take(window, source_ids, axis=1)  15.9 us
    gather x15, local copies, waits for them, and re-layouts, take_rows(): gathered.append(padded[np.arange(count_nodes) + shift_by + pad_width])  15.6 us
    dot_general x8, matrix products, add_block(): jnp.einsum('qs,qhg->hsg', selection_mask, contribution, precision=EXACT_A...  10.5 us
    dot_general x5, matrix products, couple_level(): jnp.einsum('navr,nras->nvs', sources, blocks, precision=EXACT_ARITHMETIC)  7.84 us
  transfers between devices with their start and end apart: 14, of which 1 were waited for; matrix products, arithmetic and copies ran while one was open for 48% of the time, Pallas kernels for 0%

commit v1 on v0

--- a/solution.py
+++ b/solution.py
@@ -148,6 +148,26 @@
 
 
 def on_device(vectors, coords, leaf_basis, node_ops, top_ops, near_target, near_source, near_count):
+
+    def _group_leaf(x_in, dim_at):
+        degree = lax.axis_size("leaf")
+        found = []
+        kk = 0
+        while kk < degree:
+            found.append((kk, (kk + 1) % degree))
+            kk = kk + 1
+
+        def connect_kinds(f_now):
+            if len(f_now) == degree:
+                return f_now
+            extra = connect_kinds([lax.ppermute(f_now[0], axis_name="leaf", perm=found), *f_now])
+            return extra
+
+        right_arr = connect_kinds([x_in])
+        then = jnp.concatenate(right_arr, axis=dim_at)
+        inter = jnp.roll(then, shift=(lax.axis_index("leaf") + 1) * x_in.shape[dim_at], axis=dim_at)
+        return inter
+
     rank_size = leaf_basis.shape[0]
     columns_dev = vectors.shape[0]
     points_dev = vectors.shape[1]
@@ -200,7 +220,7 @@
         nodes_here //= 2
     top_levels = top_ops.shape[0]
     top_fields = []
-    all_roots = lax.all_gather(current, "leaf", axis=0, tiled=True)
+    all_roots = _group_leaf(current, 0)
     for height in range(top_levels):
         padded_top = jnp.pad(all_roots, ((3, 3), (0, 0), (0, 0)))
         node_id = device // (1 << height)

time: 217 us -> 303 us (1.40)
  other arithmetic: 9.62 us -> 45.1 us
  blocking collectives: 52.8 us -> 21.4 us
  local copies, waits for them, and re-layouts: 52.2 us -> 83.3 us
  waiting for transfers between devices: 3.15 us -> 31.2 us
  starting transfers between devices: 33.5 us -> 45.2 us
  matrix products: 48 us -> 56.9 us
    all_gather x1 -> x0, blocking collectives: 31.5 us -> none  [on_device(): all_roots = lax.all_gather(current, 'leaf', axis=0, tiled=True)]
    reduce_scatter x1, waiting for transfers between devices: 3.09 us -> 20.3 us  [on_device(): lax.psum_scatter(partial_sum, 'vec', scatter_dimension=0, tiled=True)]
    ppermute x0 -> x7, starting transfers between devices: none -> 13.2 us  [connect_kinds(): lax.ppermute(f_now[0], axis_name='leaf', perm=found)]
    select_n x16, other arithmetic: 0.76 us -> 10.9 us  [add_block(): source_rows = jnp.take(window, source_ids, axis=1)]
    and x8, other arithmetic: 0.13 us -> 9.75 us  [add_block(): target_pts = jnp.take(local_coords, target_ids, axis=1)]
    gather x8, local copies, waits for them, and re-layouts: 4.59 us -> 11.8 us  [add_block(): target_pts = jnp.take(local_coords, target_ids, axis=1)]
    unnamed x60 -> x100, local copies, waits for them, and re-layouts: 5.28 us -> 11.3 us
    ppermute x0 -> x7, waiting for transfers between devices: none -> 5.8 us  [connect_kinds(): lax.ppermute(f_now[0], axis_name='leaf', perm=found)]
  transfers between devices with their start and end apart: 14 -> 21, of which waited for: 1 -> 5; matrix products, arithmetic and copies ran while one was open for 48% -> 24% of each run, Pallas kernels for 0% -> 0%
where the time goes in v1:
time: 303 us; the launch traced here: 300 us
  local copies, waits for them, and re-layouts  83.3 us (27%)
  matrix products  56.9 us (19%)
  starting transfers between devices  45.2 us (15%)
  other arithmetic  45.1 us (15%)
  waiting for transfers between devices  31.2 us (10%)
  blocking collectives  21.4 us (7%)
  between operations  15.5 us (5%)
    ppermute x6, starting transfers between devices, padded_2(): lax.ppermute(lax.slice_in_dim(block, block.shape[dim] - width, None, axis...  24.1 us
    psum x1, blocking collectives, on_device(): gram_matrix = lax.psum(gram_part, 'leaf') / (leaf_count * points_dev)  21.4 us
    gather x15, local copies, waits for them, and re-layouts, take_rows(): gathered.append(padded[np.arange(count_nodes) + shift_by + pad_width])  21 us
    reduce_scatter x1, waiting for transfers between devices, on_device(): lax.psum_scatter(partial_sum, 'vec', scatter_dimension=0, tiled=True)  20.3 us
    dot_general x8, matrix products, add_block(): jnp.einsum('vbs,bts->bvt', source_rows[:columns], kernel, precision=EXACT...  19.2 us
    gather x8, local copies, waits for them, and re-layouts, add_block(): source_rows = jnp.take(window, source_ids, axis=1)  15.9 us
    dot_general x8, matrix products, add_block(): jnp.einsum('qs,qhg->hsg', selection_mask, contribution, precision=EXACT_A...  15.4 us
    ppermute x7, starting transfers between devices, connect_kinds(): lax.ppermute(f_now[0], axis_name='leaf', perm=found)  13.2 us
  transfers between devices with their start and end apart: 21, of which 5 were waited for; matrix products, arithmetic and copies ran while one was open for 24% of the time, Pallas kernels for 0%

profile of v1, /device:TPU:0, one launch (start us, length us, event | category | flops | bytes accessed | tf_op | source)
XLA Modules:
  0.0 299.6 jit_solution(9275663300006718576)
XLA Ops:
  7.2 2.3 fusion.55
  11.4 5.5 %collective-permute-start.10 = (f32[2,8,32]{2,1,0:T(8,128)S(1)}, f32[2,8,32]{2,1,0:T(8,128)}, u32[]{:S(2)}, u32[]{:S(2)}) collective-permute-start(f32[2,8,32]{2,1,0:T(8,128)S(1)} %slice_add_fusion.3), channel_id=1, source_target_pairs={{0,4},{4,8},{8,12},{12,16},{16,20},{20,24},{24,28},{1,5},{5,9},{9,... | collective-permute-start | bytes 6152 | tf_op jit(solution)/shard_map/ppermute | solution.py:22
  19.1 2.6 collective-permute-start.12
  22.3 4.4 %collective-permute-start.8 = (f32[3,8,32]{2,1,0:T(8,128)}, f32[3,8,32]{2,1,0:T(8,128)}, u32[]{:S(2)}, u32[]{:S(2)}) collective-permute-start(f32[3,8,32]{2,1,0:T(8,128)} %get-tuple-element.106), channel_id=1, source_target_pairs={{0,4},{4,8},{8,12},{12,16},{16,20},{20,24},{24,28},{1,5},{5,9},{9,... | collective-permute-start | bytes 9224 | tf_op jit(solution)/shard_map/ppermute | solution.py:22
  43.6 3.1 %reshape.157 = f32[32,32,3,32]{3,2,1,0:T(4,128)} reshape(f32[32,32,96]{2,1,0:T(8,128)} %slice.211) | data formatting | bytes 786432 | tf_op jit(solution)/shard_map/reshape | solution.py:52
  51.7 5.1 %collective-permute-start.6 = (f32[3,8,32]{2,1,0:T(8,128)}, f32[3,8,32]{2,1,0:T(8,128)}, u32[]{:S(2)}, u32[]{:S(2)}) collective-permute-start(f32[3,8,32]{2,1,0:T(8,128)} %get-tuple-element.104), channel_id=1, source_target_pairs={{0,4},{4,8},{8,12},{12,16},{16,20},{20,24},{24,28},{1,5},{5,9},{9,... | collective-permute-start | bytes 9224 | tf_op jit(solution)/shard_map/ppermute | solution.py:22
  58.1 2.7 collective-permute-start.13
  67.3 3.1 %collective-permute-start.2 = (f32[3,8,32]{2,1,0:T(8,128)}, f32[3,8,32]{2,1,0:T(8,128)S(1)}, u32[]{:S(2)}, u32[]{:S(2)}) collective-permute-start(f32[3,8,32]{2,1,0:T(8,128)} %get-tuple-element.98), channel_id=1, source_target_pairs={{0,4},{4,8},{8,12},{12,16},{16,20},{20,24},{24,28},{1,5},{5,9},{9,... | collective-permute-start | bytes 9224 | tf_op jit(solution)/shard_map/ppermute | solution.py:22
  71.8 2.7 collective-permute-start.14
  79.1 4.0 %collective-permute-start.4 = (f32[3,8,32]{2,1,0:T(8,128)}, f32[3,8,32]{2,1,0:T(8,128)}, u32[]{:S(2)}, u32[]{:S(2)}) collective-permute-start(f32[3,8,32]{2,1,0:T(8,128)} %get-tuple-element.100), channel_id=1, source_target_pairs={{0,4},{4,8},{8,12},{12,16},{16,20},{20,24},{24,28},{1,5},{5,9},{9,... | collective-permute-start | bytes 9224 | tf_op jit(solution)/shard_map/ppermute | solution.py:22
  85.0 2.6 collective-permute-start.15
  92.5 4.7 %fusion.46 = f32[32,8,32]{2,1,0:T(8,128)} fusion(f32[32,32,3,32]{3,2,1,0:T(4,128)} %reshape.157, f32[32,1,8,32]{3,2,0,1:T(8,128)} %bitcast.181, f32[32,1,8,32]{3,2,0,1:T(8,128)} %bitcast.180, f32[32,1,8,32]{3,2,0,1:T(8,128)} %bitcast.182), kind=kOutput, calls=%fused_computation.89 | convolution fusion | flops 9486336 | bytes 524288 | tf_op jit(solution)/shard_map/navr,nras->nvs/dot_general | solution.py:53
  97.2 2.1 convolution_bitcast_fusion.2
  99.3 1.8 collective-permute-start.16
  105.4 2.0 gather_fusion.14
  108.2 1.7 convolution_bitcast_fusion.3
  109.9 4.0 %collective-permute-done.17 = f32[1,8,32]{2,1,0:T(8,128)} collective-permute-done((f32[1,8,32]{2,1,0:T(8,128)S(1)}, f32[1,8,32]{2,1,0:T(8,128)}, u32[]{:S(2)}, u32[]{:S(2)}) %collective-permute-start.17) | collective-permute-done | bytes 1056 | tf_op jit(solution)/shard_map/ppermute | solution.py:163
  118.6 1.8 collective-permute-done.18
  129.6 1.9 collective-permute-start
  134.3 4.4 %collective-permute-done.1 = f32[35,1024]{1,0:T(8,128)S(1)} collective-permute-done((f32[35,1024]{1,0:T(8,128)S(1)}, f32[35,1024]{1,0:T(8,128)S(1)}, u32[]{:S(2)}, u32[]{:S(2)}) %collective-permute-start.1) | collective-permute-done | bytes 143392 | tf_op jit(solution)/shard_map/ppermute | solution.py:25
  139.5 1.6 copy.57
  141.1 100.8 %while.11 = (s32[]{:T(128)}, f32[32,32,256]{2,1,0:T(8,128)S(1)}, s32[8,5]{1,0:T(8,128)}, f32[35,40,256]{2,0,1:T(8,128)}, s32[8,5]{1,0:T(8,128)}, /*index=5*/f32[...) while((s32[]{:T(128)}, f32[32,32,256]{2,1,0:T(8,128)S(1)}, ...), condition=%wide.region_1.2_spmd.clone, body=%wide.region_0.1_spmd.clone.sunk | while | flops 146720672 | bytes 3940823 | solution.py:146
  142.4 2.0 gather_fusion
  148.6 2.4 fusion.205
  151.8 1.9 fusion.207
  155.0 2.0 gather_fusion
  161.2 2.4 fusion.205
  164.4 1.9 fusion.207
  167.6 2.0 gather_fusion
  173.8 2.4 fusion.205
  177.0 1.9 fusion.207
  180.2 2.0 gather_fusion
  186.4 2.4 fusion.205
  189.6 1.9 fusion.207
  192.8 2.0 gather_fusion
  199.0 2.4 fusion.205
  202.2 1.9 fusion.207
  205.4 2.0 gather_fusion
  211.6 2.4 fusion.205
  214.8 1.9 fusion.207
  218.0 2.0 gather_fusion
  224.2 2.4 fusion.205
  227.4 1.9 fusion.207
  230.6 2.0 gather_fusion
  236.8 2.4 fusion.205
  240.0 1.9 fusion.207
  248.5 20.3 %reduce-scatter.2.cloned.1.call-done = f32[8,8192]{1,0:T(8,128)} async-done(((f32[32,8192]{1,0:T(8,128)}), f32[8,8192]{1,0:T(8,128)}) %reduce-scatter.2.cloned.1.call-update) | async-done | bytes 262160 | tf_op jit(solution)/shard_map/reduce_scatter | solution.py:200
  270.7 21.4 %psum.7 = f32[32,8]{0,1:T(8,128)S(1)} all-reduce(f32[32,8]{0,1:T(8,128)S(1)} %convolution_bitcast_fusion.5), channel_id=1, replica_groups=mesh['leaf'=8,'vec'=4] {'leaf'}, use_global_device_ids=true, to_apply=%region_3.4 | all-reduce | flops 256 | bytes 2048 | tf_op jit(solution)/shard_map/psum | solution.py:246
  (373 shorter events, 126.4 us)
Async XLA Ops:
  7.2 121.0 %all-gather.2.cloned.1.call-start = ((), (), s32[]{:S(2)}) async-start(), calls=%async_computation.1 | async-start | bytes 1310720 | tf_op jit(solution)/shard_map/all_gather | solution.py:179
  9.5 20.3 %copy-start.19 = (f32[2,32,192]{2,1,0:T(8,128)S(1)}, f32[2,32,192]{2,1,0:T(8,128)}, u32[]{:S(2)}) copy-start(f32[2,32,192]{2,1,0:T(8,128)} %param.44) | copy-start | bytes 147460
  9.6 21.6 %copy-start.41 = (s32[4]{0:T(128)S(1)}, s32[4]{0:T(128)}, u32[]{:S(2)}) copy-start(s32[4]{0:T(128)} %constant.235) | copy-start | bytes 52
  9.6 22.2 %copy-start.40 = (s32[8]{0:T(128)S(1)}, s32[8]{0:T(128)}, u32[]{:S(2)}) copy-start(s32[8]{0:T(128)} %constant.232) | copy-start | bytes 100
  9.6 22.7 %copy-start.39 = (s32[16]{0:T(128)S(1)}, s32[16]{0:T(128)}, u32[]{:S(2)}) copy-start(s32[16]{0:T(128)} %constant.229) | copy-start | bytes 196
  9.6 23.3 %copy-start.38 = (s32[32]{0:T(128)S(1)}, s32[32]{0:T(128)}, u32[]{:S(2)}) copy-start(s32[32]{0:T(128)} %constant.226) | copy-start | bytes 388
  9.6 25.2 %copy-start.37 = (s32[2]{0:T(128)S(1)}, s32[2]{0:T(128)}, u32[]{:S(2)}) copy-start(s32[2]{0:T(128)} %constant.238) | copy-start | bytes 28
  9.6 25.8 %copy-start.35 = (s32[4]{0:T(128)S(1)}, s32[4]{0:T(128)}, u32[]{:S(2)}) copy-start(s32[4]{0:T(128)} %constant.236) | copy-start | bytes 52
  9.6 25.8 %copy-start.36 = (s32[4]{0:T(128)S(1)}, s32[4]{0:T(128)}, u32[]{:S(2)}) copy-start(s32[4]{0:T(128)} %constant.237) | copy-start | bytes 52
  9.6 26.4 %copy-start.33 = (s32[8]{0:T(128)S(1)}, s32[8]{0:T(128)}, u32[]{:S(2)}) copy-start(s32[8]{0:T(128)} %constant.233) | copy-start | bytes 100
  9.7 26.4 %copy-start.34 = (s32[8]{0:T(128)S(1)}, s32[8]{0:T(128)}, u32[]{:S(2)}) copy-start(s32[8]{0:T(128)} %constant.234) | copy-start | bytes 100
  9.7 26.9 %copy-start.31 = (s32[16]{0:T(128)S(1)}, s32[16]{0:T(128)}, u32[]{:S(2)}) copy-start(s32[16]{0:T(128)} %constant.230) | copy-start | bytes 196
  9.7 26.9 %copy-start.32 = (s32[16]{0:T(128)S(1)}, s32[16]{0:T(128)}, u32[]{:S(2)}) copy-start(s32[16]{0:T(128)} %constant.231) | copy-start | bytes 196
  9.7 27.5 %copy-start.29 = (s32[32]{0:T(128)S(1)}, s32[32]{0:T(128)}, u32[]{:S(2)}) copy-start(s32[32]{0:T(128)} %constant.227) | copy-start | bytes 388
  9.7 27.5 %copy-start.30 = (s32[32]{0:T(128)S(1)}, s32[32]{0:T(128)}, u32[]{:S(2)}) copy-start(s32[32]{0:T(128)} %constant.228) | copy-start | bytes 388
  9.7 28.1 %copy-start.27 = (s32[160]{0:T(256)S(1)}, s32[160]{0:T(256)}, u32[]{:S(2)}) copy-start(s32[160]{0:T(256)} %param.46) | copy-start | bytes 1924
  9.7 28.1 %copy-start.28 = (s32[160]{0:T(256)S(1)}, s32[160]{0:T(256)}, u32[]{:S(2)}) copy-start(s32[160]{0:T(256)} %param.45) | copy-start | bytes 1924
  11.4 45.4 %collective-permute-start.10 = (f32[2,8,32]{2,1,0:T(8,128)S(1)}, f32[2,8,32]{2,1,0:T(8,128)}, u32[]{:S(2)}, u32[]{:S(2)}) collective-permute-start(f32[2,8,32]{2,1,0:T(8,128)S(1)} %slice_add_fusion.3), channel_id=1, source_target_pairs={{0,4},{4,8},{8,12},{12,16},{16,20},{20,24},{24,28},{1,5},{5,9},{9,... | collective-permute-start | bytes 6152 | tf_op jit(solution)/shard_map/ppermute | solution.py:22
  16.9 41.2 %collective-permute-start.11 = (f32[2,8,32]{2,1,0:T(8,128)S(1)}, f32[2,8,32]{2,1,0:T(8,128)}, u32[]{:S(2)}, u32[]{:S(2)}) collective-permute-start(f32[2,8,32]{2,1,0:T(8,128)S(1)} %slice_add_fusion.3), channel_id=1, source_target_pairs={{4,0},{8,4},{12,8},{16,12},{20,16},{24,20},{28,24},{5,1},{9,5},{13... | collective-permute-start | bytes 6152 | tf_op jit(solution)/shard_map/ppermute | solution.py:25
  18.2 250.6 %reduce-scatter.2.cloned.1.call-start = ((), (), s32[]{:S(2)}) async-start(), calls=%async_computation.2 | async-start | bytes 1310720 | tf_op jit(solution)/shard_map/reduce_scatter | solution.py:200
  18.5 20.1 %copy-start.16 = (f32[2,8,32]{2,1,0:T(8,128)}, f32[2,8,32]{2,1,0:T(8,128)S(1)}, u32[]{:S(2)}) copy-start(f32[2,8,32]{2,1,0:T(8,128)S(1)} %fusion.97) | copy-start | bytes 6148
  19.1 32.6 %collective-permute-start.12 = (f32[1,8,32]{2,1,0:T(8,128)}, f32[1,8,32]{2,1,0:T(8,128)S(1)}, u32[]{:S(2)}, u32[]{:S(2)}) collective-permute-start(f32[1,8,32]{2,1,0:T(8,128)} %slice_add_fusion.4), channel_id=1, source_target_pairs={{0,4},{4,8},{8,12},{12,16},{16,20},{20,24},{24,28},{28,0},{1,5},{5... | collective-permute-start | bytes 3080 | tf_op jit(solution)/shard_map/ppermute | solution.py:163
  22.3 78.8 %collective-permute-start.8 = (f32[3,8,32]{2,1,0:T(8,128)}, f32[3,8,32]{2,1,0:T(8,128)}, u32[]{:S(2)}, u32[]{:S(2)}) collective-permute-start(f32[3,8,32]{2,1,0:T(8,128)} %get-tuple-element.106), channel_id=1, source_target_pairs={{0,4},{4,8},{8,12},{12,16},{16,20},{20,24},{24,28},{1,5},{5,9},{9,... | collective-permute-start | bytes 9224 | tf_op jit(solution)/shard_map/ppermute | solution.py:22
  26.7 74.5 %collective-permute-start.9 = (f32[3,8,32]{2,1,0:T(8,128)}, f32[3,8,32]{2,1,0:T(8,128)}, u32[]{:S(2)}, u32[]{:S(2)}) collective-permute-start(f32[3,8,32]{2,1,0:T(8,128)} %get-tuple-element.107), channel_id=1, source_target_pairs={{4,0},{8,4},{12,8},{16,12},{20,16},{24,20},{28,24},{5,1},{9,5},{13... | collective-permute-start | bytes 9224 | tf_op jit(solution)/shard_map/ppermute | solution.py:25
  46.8 19.6 %copy-start.10 = (f32[2,32,3,32]{3,2,1,0:T(4,128)S(1)}, f32[2,32,3,32]{3,2,1,0:T(4,128)}, u32[]{:S(2)}) copy-start(f32[2,32,3,32]{3,2,1,0:T(4,128)} %reshape.161) | copy-start | bytes 73732
  51.7 32.7 %copy-start.22 = (f32[1,8,32]{2,1,0:T(8,128)}, f32[1,8,32]{2,1,0:T(8,128)S(1)}, u32[]{:S(2)}) copy-start(f32[1,8,32]{2,1,0:T(8,128)S(1)} %collective-permute-done.12) | copy-start | bytes 3076
  51.7 18.8 %collective-permute-start.6 = (f32[3,8,32]{2,1,0:T(8,128)}, f32[3,8,32]{2,1,0:T(8,128)}, u32[]{:S(2)}, u32[]{:S(2)}) collective-permute-start(f32[3,8,32]{2,1,0:T(8,128)} %get-tuple-element.104), channel_id=1, source_target_pairs={{0,4},{4,8},{8,12},{12,16},{16,20},{20,24},{24,28},{1,5},{5,9},{9,... | collective-permute-start | bytes 9224 | tf_op jit(solution)/shard_map/ppermute | solution.py:22
  56.8 14.9 %collective-permute-start.7 = (f32[3,8,32]{2,1,0:T(8,128)}, f32[3,8,32]{2,1,0:T(8,128)}, u32[]{:S(2)}, u32[]{:S(2)}) collective-permute-start(f32[3,8,32]{2,1,0:T(8,128)} %get-tuple-element.105), channel_id=1, source_target_pairs={{4,0},{8,4},{12,8},{16,12},{20,16},{24,20},{28,24},{5,1},{9,5},{13... | collective-permute-start | bytes 9224 | tf_op jit(solution)/shard_map/ppermute | solution.py:25
  58.1 9.2 %collective-permute-start.13 = (f32[1,8,32]{2,1,0:T(8,128)S(1)}, f32[1,8,32]{2,1,0:T(8,128)}, u32[]{:S(2)}, u32[]{:S(2)}) collective-permute-start(f32[1,8,32]{2,1,0:T(8,128)S(1)} %collective-permute-done.12), channel_id=1, source_target_pairs={{0,4},{4,8},{8,12},{12,16},{16,20},{20,24},{24,28},{28,0},{1,5},{5... | collective-permute-start | bytes 3080 | tf_op jit(solution)/shard_map/ppermute | solution.py:163
  67.3 15.8 %collective-permute-start.2 = (f32[3,8,32]{2,1,0:T(8,128)}, f32[3,8,32]{2,1,0:T(8,128)S(1)}, u32[]{:S(2)}, u32[]{:S(2)}) collective-permute-start(f32[3,8,32]{2,1,0:T(8,128)} %get-tuple-element.98), channel_id=1, source_target_pairs={{0,4},{4,8},{8,12},{12,16},{16,20},{20,24},{24,28},{1,5},{5,9},{9,... | collective-permute-start | bytes 9224 | tf_op jit(solution)/shard_map/ppermute | solution.py:22
  70.4 13.9 %collective-permute-start.3 = (f32[3,8,32]{2,1,0:T(8,128)}, f32[3,8,32]{2,1,0:T(8,128)S(1)}, u32[]{:S(2)}, u32[]{:S(2)}) collective-permute-start(f32[3,8,32]{2,1,0:T(8,128)} %get-tuple-element.99), channel_id=1, source_target_pairs={{4,0},{8,4},{12,8},{16,12},{20,16},{24,20},{28,24},{5,1},{9,5},{13... | collective-permute-start | bytes 9224 | tf_op jit(solution)/shard_map/ppermute | solution.py:25
  71.8 7.3 %collective-permute-start.14 = (f32[1,8,32]{2,1,0:T(8,128)}, f32[1,8,32]{2,1,0:T(8,128)}, u32[]{:S(2)}, u32[]{:S(2)}) collective-permute-start(f32[1,8,32]{2,1,0:T(8,128)} %collective-permute-done.13), channel_id=1, source_target_pairs={{0,4},{4,8},{8,12},{12,16},{16,20},{20,24},{24,28},{28,0},{1,5},{5... | collective-permute-start | bytes 3080 | tf_op jit(solution)/shard_map/ppermute | solution.py:163
  79.1 34.9 %collective-permute-start.4 = (f32[3,8,32]{2,1,0:T(8,128)}, f32[3,8,32]{2,1,0:T(8,128)}, u32[]{:S(2)}, u32[]{:S(2)}) collective-permute-start(f32[3,8,32]{2,1,0:T(8,128)} %get-tuple-element.100), channel_id=1, source_target_pairs={{0,4},{4,8},{8,12},{12,16},{16,20},{20,24},{24,28},{1,5},{5,9},{9,... | collective-permute-start | bytes 9224 | tf_op jit(solution)/shard_map/ppermute | solution.py:22
  83.1 30.8 %collective-permute-start.5 = (f32[3,8,32]{2,1,0:T(8,128)}, f32[3,8,32]{2,1,0:T(8,128)}, u32[]{:S(2)}, u32[]{:S(2)}) collective-permute-start(f32[3,8,32]{2,1,0:T(8,128)} %get-tuple-element.101), channel_id=1, source_target_pairs={{4,0},{8,4},{12,8},{16,12},{20,16},{24,20},{28,24},{5,1},{9,5},{13... | collective-permute-start | bytes 9224 | tf_op jit(solution)/shard_map/ppermute | solution.py:25
  85.0 14.3 %collective-permute-start.15 = (f32[1,8,32]{2,1,0:T(8,128)}, f32[1,8,32]{2,1,0:T(8,128)}, u32[]{:S(2)}, u32[]{:S(2)}) collective-permute-start(f32[1,8,32]{2,1,0:T(8,128)} %collective-permute-done.14), channel_id=1, source_target_pairs={{0,4},{4,8},{8,12},{12,16},{16,20},{20,24},{24,28},{28,0},{1,5},{5... | collective-permute-start | bytes 3080 | tf_op jit(solution)/shard_map/ppermute | solution.py:163
  92.5 4.7 %copy-start.4 = (f32[8,32,3,32]{3,2,1,0:T(4,128)S(1)}, f32[8,32,3,32]{3,2,1,0:T(4,128)}, u32[]{:S(2)}) copy-start(f32[8,32,3,32]{3,2,1,0:T(4,128)} %reshape.159) | copy-start | bytes 294916
  92.5 15.7 %copy-start.6 = (f32[4,32,3,32]{3,2,1,0:T(4,128)S(1)}, f32[4,32,3,32]{3,2,1,0:T(4,128)}, u32[]{:S(2)}) copy-start(f32[4,32,3,32]{3,2,1,0:T(4,128)} %reshape.160) | copy-start | bytes 147460
  97.2 25.9 %copy-start.23 = (f32[1,8,32]{2,1,0:T(8,128)S(1)}, f32[1,8,32]{2,1,0:T(8,128)}, u32[]{:S(2)}) copy-start(f32[1,8,32]{2,1,0:T(8,128)} %copy-done.22) | copy-start | bytes 3076
  97.2 25.9 %copy-start.17 = (f32[2,8,32]{2,1,0:T(8,128)S(1)}, f32[2,8,32]{2,1,0:T(8,128)}, u32[]{:S(2)}) copy-start(f32[2,8,32]{2,1,0:T(8,128)} %copy-done.16) | copy-start | bytes 6148
  97.2 29.0 %copy-start.11 = (f32[32,192]{1,0:T(8,128)S(1)}, f32[32,192]{1,0:T(8,128)}, u32[]{:S(2)}) copy-start(f32[32,192]{1,0:T(8,128)} %get-tuple-element.102) | copy-start | bytes 73732
  99.3 8.1 %collective-permute-start.16 = (f32[1,8,32]{2,1,0:T(8,128)}, f32[1,8,32]{2,1,0:T(8,128)S(1)}, u32[]{:S(2)}, u32[]{:S(2)}) collective-permute-start(f32[1,8,32]{2,1,0:T(8,128)} %collective-permute-done.15), channel_id=1, source_target_pairs={{0,4},{4,8},{8,12},{12,16},{16,20},{20,24},{24,28},{28,0},{1,5},{5... | collective-permute-start | bytes 3080 | tf_op jit(solution)/shard_map/ppermute | solution.py:163
  107.5 6.4 %collective-permute-start.17 = (f32[1,8,32]{2,1,0:T(8,128)S(1)}, f32[1,8,32]{2,1,0:T(8,128)}, u32[]{:S(2)}, u32[]{:S(2)}) collective-permute-start(f32[1,8,32]{2,1,0:T(8,128)S(1)} %collective-permute-done.16), channel_id=1, source_target_pairs={{0,4},{4,8},{8,12},{12,16},{16,20},{20,24},{24,28},{28,0},{1,5},{5... | collective-permute-start | bytes 3080 | tf_op jit(solution)/shard_map/ppermute | solution.py:163
  113.9 6.5 %collective-permute-start.18 = (f32[1,8,32]{2,1,0:T(8,128)}, f32[1,8,32]{2,1,0:T(8,128)S(1)}, u32[]{:S(2)}, u32[]{:S(2)}) collective-permute-start(f32[1,8,32]{2,1,0:T(8,128)} %collective-permute-done.17), channel_id=1, source_target_pairs={{0,4},{4,8},{8,12},{12,16},{16,20},{20,24},{24,28},{28,0},{1,5},{5... | collective-permute-start | bytes 3080 | tf_op jit(solution)/shard_map/ppermute | solution.py:163
  129.6 4.7 %collective-permute-start = (f32[35,1024]{1,0:T(8,128)S(1)}, f32[35,1024]{1,0:T(8,128)S(1)}, u32[]{:S(2)}, u32[]{:S(2)}) collective-permute-start(f32[35,1024]{1,0:T(8,128)S(1)} %get-tuple-element.96), channel_id=1, source_target_pairs={{0,4},{4,8},{8,12},{12,16},{16,20},{20,24},{24,28},{1,5},{5,9},{9,... | collective-permute-start | bytes 430088 | tf_op jit(solution)/shard_map/ppermute | solution.py:22
  131.5 7.2 %collective-permute-start.1 = (f32[35,1024]{1,0:T(8,128)S(1)}, f32[35,1024]{1,0:T(8,128)S(1)}, u32[]{:S(2)}, u32[]{:S(2)}) collective-permute-start(f32[35,1024]{1,0:T(8,128)S(1)} %get-tuple-element.97), channel_id=1, source_target_pairs={{4,0},{8,4},{12,8},{16,12},{20,16},{24,20},{28,24},{5,1},{9,5},{13... | collective-permute-start | bytes 430088 | tf_op jit(solution)/shard_map/ppermute | solution.py:25
  246.8 22.0 %copy-start.3 = (f32[8,8192]{1,0:T(8,128)S(1)}, f32[8,8192]{1,0:T(8,128)}, u32[]{:S(2)}) copy-start(f32[8,8192]{1,0:T(8,128)} %param.40) | copy-start | bytes 786436
  247.8 22.0 %copy-start.1 = (f32[32,8192]{1,0:T(8,128)S(1)}, f32[32,8192]{1,0:T(8,128)}, u32[]{:S(2)}) copy-start(f32[32,8192]{1,0:T(8,128)} %all-gather.2.cloned.1.call-done) | copy-start | bytes 3145732
  269.8 22.9 %copy-start.5 = (f32[8,8192]{1,0:T(8,128)}, f32[8,8192]{1,0:T(8,128)S(1)}, u32[]{:S(2)}) copy-start(f32[8,8192]{1,0:T(8,128)S(1)} %multiply_add_fusion) | copy-start | bytes 786436
  (22 other events, 51.8 us)
Sparse Core Ops, SparseCore 0:
  18.3 19.1 all-gather.1
  243.7 25.0 reduce-scatter.1
